TPU v7x, 256 devices: a whole 4x4x8 slice. The times are simulated.
256 devices in a mesh: rep: 4 (over y), fsdp: 64 (over x, z, core).
Axes of the slice: x: 4, y: 4, z: 8, core: 2. Of those that a mesh axis runs over, the one named last changes fastest.
Arguments:
- grad_blocks: bfloat16 [4, 64, 512, 512], P('rep', None, 'fsdp'), may hold values from -6 to 6
- graft_accum: float32 [64, 512, 512], P(None, 'fsdp'), may hold values from 0.1 to 1000000
- left_stats: float32 [128, 512, 512], P('fsdp'), may hold values from -300000 to 300000, as said below
- right_stats: float32 [128, 512, 512], P('fsdp'), may hold values from -300000 to 300000, as said below
- block_slot: int32 [64], replicated, may hold values from 0 to 127, as said below
- vocab_grads: bfloat16 [4, 2, 512, 8192], P('rep', None, 'fsdp'), may hold values from -6 to 6
- vocab_accum: float32 [2, 512, 8192], P(None, 'fsdp'), may hold values from 0.01 to 10
Outputs:
- direction: bfloat16 [64, 512, 512], P(None, 'fsdp')
- graft_accum_new: float32 [64, 512, 512], P(None, 'fsdp')
- left_new: float32 [128, 512, 512], P('fsdp')
- right_new: float32 [128, 512, 512], P('fsdp')
- vocab_accum_new: float32 [2, 512, 8192], P(None, 'fsdp')
- vocab_step: bfloat16 [2, 512, 8192], P(None, 'fsdp')
Inputs may be any that keep to these rules, and one draw needn't show every extreme that they name: Block b's statistics sit in slot block_slot[b]; slot s belongs to fsdp index s // 2; no two blocks name the same slot; every fsdp index owns at most 2 blocks and some index owns exactly 2. `left_stats`: every slot holds a symmetric positive definite matrix. `right_stats`: every slot holds a symmetric positive definite matrix.
All inputs are finite; a program needn't handle non-finite values.
Results may differ from a plain program's by a relative error of at most 0.017.
Values may be sent and summed in bfloat16 or wider, within the bound.
A program may use at most 64 MiB of HBM per device.

v0:
```python
import jax
import jax.numpy as jnp
from jax import lax
from jax.sharding import PartitionSpec as P

ITERS = 6


def as_sent(shard):

    def short(part):
        return part.astype(jnp.bfloat16) if part.dtype == jnp.float32 else part

    return jax.tree.map(short, shard)


def batch_product(left, right):
    return jnp.einsum("sij,sjk->sik", left, right, precision=lax.Precision.HIGHEST)


def batch_root(matrices):
    matrix_order = matrices.shape[-1]
    identity = jnp.eye(matrix_order, dtype=jnp.float32)[None]
    frobenius = jnp.sqrt(jnp.sum(matrices * matrices, axis=(1, 2)))
    scaled = matrices / frobenius[:, None, None]
    result = identity
    for iteration in range(ITERS):
        factor = (5.0 * identity - scaled) * 0.25
        result = factor if iteration == 0 else batch_product(result, factor)
        if iteration + 1 < ITERS:
            square = batch_product(factor, factor)
            fourth = batch_product(square, square)
            scaled = batch_product(fourth, scaled)
    return result


def on_device(
    grad_blocks, graft_accum, left_stats, right_stats, block_slot, vocab_grads, vocab_accum
):
    summed_grad, summed_vocab = (
        lax.psum(grad_blocks[0].astype(jnp.float32).astype(jnp.bfloat16), "rep").astype(
            jnp.float32
        ),
        lax.psum(vocab_grads[0].astype(jnp.float32).astype(jnp.bfloat16), "rep").astype(
            jnp.float32
        ),
    )
    grad_sum = summed_grad.astype(jnp.bfloat16)
    vocab_sum = summed_vocab.astype(jnp.bfloat16)
    vocab_float = vocab_sum.astype(jnp.float32)
    vocab_accum_new = vocab_accum + vocab_float * vocab_float
    vocab_step = (vocab_float / (jnp.sqrt(vocab_accum_new) + 1e-10)).astype(jnp.bfloat16)
    grad_float = grad_sum.astype(jnp.float32)
    graft_accum_new = graft_accum + grad_float * grad_float
    grafted = grad_float / (jnp.sqrt(graft_accum_new) + 1e-10)
    graft_part = jnp.sum(grafted * grafted, axis=(1, 2))
    matrix_order = grad_blocks.shape[-1]
    entries = float(matrix_order * matrix_order)
    slot_count = left_stats.shape[0]
    total_slots = slot_count * lax.axis_size("fsdp")
    onehot = (block_slot[None, :] == jnp.arange(total_slots, dtype=jnp.int32)[:, None]).astype(
        jnp.bfloat16
    )
    outgoing = jnp.einsum(
        "sb,brc->src", onehot, grad_sum, preferred_element_type=jnp.float32
    ).astype(jnp.bfloat16)
    received = lax.all_to_all(outgoing, "fsdp", split_axis=0, concat_axis=1, tiled=True)
    left_new = left_stats + jnp.einsum(
        "sij,skj->sik", received, received, preferred_element_type=jnp.float32
    )
    right_new = right_stats + jnp.einsum(
        "sji,sjk->sik", received, received, preferred_element_type=jnp.float32
    )
    stacked = jnp.concatenate([left_new, right_new], axis=0)
    share_count = stacked.shape[0] // lax.axis_size("rep")
    own_share = lax.dynamic_slice_in_dim(
        stacked, lax.axis_index("rep") * share_count, share_count, 0
    )
    inverse_roots = lax.all_gather(
        batch_root(own_share).astype(jnp.bfloat16), "rep", axis=0, tiled=True
    ).astype(jnp.float32)
    block_float = received.astype(jnp.float32)
    shampoo = batch_product(
        batch_product(inverse_roots[:slot_count], block_float), inverse_roots[slot_count:]
    )
    returned = lax.all_to_all(
        as_sent(shampoo), "fsdp", split_axis=1, concat_axis=0, tiled=True
    ).astype(shampoo.dtype)
    shampoo_rows = jnp.take(returned, block_slot, axis=0)
    shampoo_part = jnp.sum(shampoo_rows * shampoo_rows, axis=(1, 2))
    graft_total, shampoo_total = lax.psum((graft_part, shampoo_part), "fsdp")
    graft_scale = jnp.sqrt(graft_total / entries) / jnp.sqrt(shampoo_total / entries + 1e-06)
    direction = (shampoo_rows * graft_scale[:, None, None]).astype(jnp.bfloat16)
    return (direction, graft_accum_new, left_new, right_new, vocab_accum_new, vocab_step)


def solution(mesh):
    in_specs = (
        P("rep", None, "fsdp", None),
        P(None, "fsdp", None),
        P("fsdp", None, None),
        P("fsdp", None, None),
        P(),
        P("rep", None, "fsdp", None),
        P(None, "fsdp", None),
    )
    out_specs = (
        P(None, "fsdp", None),
        P(None, "fsdp", None),
        P("fsdp", None, None),
        P("fsdp", None, None),
        P(None, "fsdp", None),
        P(None, "fsdp", None),
    )
    return jax.shard_map(
        on_device, mesh=mesh, in_specs=in_specs, out_specs=out_specs, check_vma=False
    )
```

profile of v0, /device:TPU:8, one launch (start us, length us, event | category | flops | bytes accessed | tf_op | source)
XLA Modules:
  0.0 361.6 jit_solution(7396740100654670768)
XLA Ops:
  7.2 2.0 copy.57
  9.2 53.5 %all-reduce.4.cloned.1.call-done = (bf16[64,8,512]{2,0,1:T(8,128)(2,1)}, bf16[2,8,8192]{2,1,0:T(8,128)(2,1)}) async-done(((bf16[64,8,512]{2,0,1:T(8,128)(2,1)}, bf16[2,8,8192]{2,1,0:T(8,128)(2,1)}), (bf16[64,8,512]{2,0,1:T(8,128)(2,1)}, bf16[2,8,8192]{2,1,0:T(8,128)(2,1)})) %all-reduce.4.cloned.1.call-update) | async-done | bytes 786448 | tf_op jit(solution)/shard_map/psum | solution.py:41
  65.9 10.4 %all-to-all-start = ((bf16[128,8,512]{2,1,0:T(8,128)(2,1)}), bf16[128,8,512]{2,1,0:T(8,128)(2,1)S(1)}, u32[]{:S(2)}, u32[]{:S(2)}) async-start(bf16[128,8,512]{2,1,0:T(8,128)(2,1)} %copy.32), calls=%async_computation | async-start | bytes 2097152 | tf_op jit(solution)/shard_map/all_to_all | solution.py:67
  77.0 27.6 %all-to-all-done = bf16[128,8,512]{2,1,0:T(8,128)(2,1)S(1)} async-done(((bf16[128,8,512]{2,1,0:T(8,128)(2,1)}), bf16[128,8,512]{2,1,0:T(8,128)(2,1)S(1)}, u32[]{:S(2)}, u32[]{:S(2)}) %all-to-all-start) | async-done | bytes 1048608 | tf_op jit(solution)/shard_map/all_to_all | solution.py:67
  104.5 2.5 convolution_add_fusion
  112.2 1.9 fusion.12
  117.8 2.0 fusion.10
  119.8 1.9 fusion.31
  123.6 2.0 fusion.104
  125.6 1.9 fusion.27
  127.5 1.9 fusion.29
  133.2 1.9 fusion.23
  135.1 1.9 fusion.25
  137.0 2.1 fusion.107
  140.9 1.9 fusion.19
  142.9 1.9 fusion.21
  146.6 1.9 fusion
  148.5 2.6 convolution_convert_fusion.2
  151.2 29.0 %all-gather.3.cloned.1.call-done = bf16[2048,512]{1,0:T(8,128)(2,1)} async-done(((bf16[512,512]{1,0:T(8,128)(2,1)}), bf16[2048,512]{1,0:T(8,128)(2,1)}) %all-gather.3.cloned.1.call-update) | async-done | bytes 2097168 | tf_op jit(solution)/shard_map/all_gather | solution.py:79
  182.6 2.1 convolution_convert_fusion.1
  184.7 2.0 copy.35
  186.8 10.4 %all-to-all-start.1 = ((bf16[2,512,512]{2,0,1:T(2,128)(2,1)}), bf16[2,512,512]{2,0,1:T(2,128)(2,1)S(1)}, u32[]{:S(2)}, u32[]{:S(2)}) async-start(bf16[2,512,512]{2,0,1:T(2,128)(2,1)} %copy.35), calls=%async_computation.1 | async-start | bytes 2097152 | tf_op jit(solution)/shard_map/all_to_all | solution.py:86
  200.8 24.6 %all-to-all-done.1 = bf16[2,512,512]{2,0,1:T(2,128)(2,1)S(1)} async-done(((bf16[2,512,512]{2,0,1:T(2,128)(2,1)}), bf16[2,512,512]{2,0,1:T(2,128)(2,1)S(1)}, u32[]{:S(2)}, u32[]{:S(2)}) %all-to-all-start.1) | async-done | bytes 1048608 | tf_op jit(solution)/shard_map/all_to_all | solution.py:86
  227.5 126.0 %all-reduce = (f32[64]{0:T(128)S(1)}, f32[64]{0:T(128)S(1)}) all-reduce(f32[64]{0:T(128)S(1)} %multiply_reduce_fusion, f32[64]{0:T(128)S(1)} %get-tuple-element.36), channel_id=1, replica_groups=mesh['rep'=4,'fsdp'=64] {'fsdp'}, use_global_device_ids=true, to_apply=%region_5.6 | all-reduce | flops 128 | bytes 1024 | tf_op jit(solution)/shard_map/psum | solution.py:91
  (46 shorter events, 30.2 us)
Async XLA Ops:
  7.2 55.6 %all-reduce.4.cloned.1.call-start = ((), (), s32[]{:S(2)}) async-start(), calls=%async_computation.3 | async-start | bytes 1572864 | tf_op jit(solution)/shard_map/psum | solution.py:41
  65.9 38.6 %all-to-all-start = ((bf16[128,8,512]{2,1,0:T(8,128)(2,1)}), bf16[128,8,512]{2,1,0:T(8,128)(2,1)S(1)}, u32[]{:S(2)}, u32[]{:S(2)}) async-start(bf16[128,8,512]{2,1,0:T(8,128)(2,1)} %copy.32), calls=%async_computation | async-start | bytes 2097152 | tf_op jit(solution)/shard_map/all_to_all | solution.py:67
  76.4 103.9 %all-gather.3.cloned.1.call-start = ((), (), s32[]{:S(2)}) async-start(), calls=%async_computation.2 | async-start | bytes 2621440 | tf_op jit(solution)/shard_map/all_gather | solution.py:79
  104.5 2.5 copy-start.2
  107.0 3.7 %copy-start = (f32[2,512,512]{2,1,0:T(8,128)}, f32[2,512,512]{2,1,0:T(8,128)S(1)}, u32[]{:S(2)}) copy-start(f32[2,512,512]{2,1,0:T(8,128)S(1)} %convolution_add_fusion) | copy-start | bytes 6291460
  107.8 1.3 copy-start.1
  148.5 2.7 copy-start.7
  184.7 12.5 %copy-start.3 = (bf16[64,8,512]{2,0,1:T(8,128)(2,1)S(1)}, bf16[64,8,512]{2,0,1:T(8,128)(2,1)}, u32[]{:S(2)}) copy-start(bf16[64,8,512]{2,0,1:T(8,128)(2,1)} %get-tuple-element.32) | copy-start | bytes 1572868
  184.7 12.5 %copy-start.4 = (f32[64,8,512]{2,1,0:T(8,128)S(1)}, f32[64,8,512]{2,1,0:T(8,128)}, u32[]{:S(2)}) copy-start(f32[64,8,512]{2,1,0:T(8,128)} %param.8) | copy-start | bytes 3145732
  186.8 38.6 %all-to-all-start.1 = ((bf16[2,512,512]{2,0,1:T(2,128)(2,1)}), bf16[2,512,512]{2,0,1:T(2,128)(2,1)S(1)}, u32[]{:S(2)}, u32[]{:S(2)}) async-start(bf16[2,512,512]{2,0,1:T(2,128)(2,1)} %copy.35), calls=%async_computation.1 | async-start | bytes 2097152 | tf_op jit(solution)/shard_map/all_to_all | solution.py:86
  197.2 2.5 copy-start.5
  197.3 2.5 copy-start.6
Sparse Core Ops, SparseCore 0:
  11.0 51.6 all-reduce.3
  151.3 28.9 all-gather.2
where the time goes:
time: 364 us; the launch traced here: 362 us
  waiting for transfers between devices  135 us (37%)
  blocking collectives  126 us (35%)
  matrix products  46.4 us (13%)
  starting transfers between devices  21.5 us (6%)
  between operations  15.4 us (4%)
  local copies, waits for them, and re-layouts  11 us (3%)
  other arithmetic  6.57 us (2%)
    psum x1, blocking collectives, on_device(): graft_total, shampoo_total = lax.psum((graft_part, shampoo_part), 'fsdp')  126 us
    psum x1, waiting for transfers between devices, on_device(): lax.psum(grad_blocks[0].astype(jnp.float32).astype(jnp.bfloat16), 'rep')  53.5 us
    dot_general x22, matrix products, batch_product(): jnp.einsum('sij,sjk->sik', left, right, precision=lax.Precision.HIGHEST)  41.6 us
    all_gather x1, waiting for transfers between devices, on_device(): lax.all_gather(batch_root(own_share).astype(jnp.bfloat16), 'rep', axis=0,...  29 us
    all_to_all x1, waiting for transfers between devices, on_device(): lax.all_to_all(outgoing, 'fsdp', split_axis=0, concat_axis=1, tiled=True)  27.6 us
    all_to_all x1, waiting for transfers between devices, on_device(): lax.all_to_all(as_sent(shampoo), 'fsdp', split_axis=1, concat_axis=0, til...  24.6 us
    all_to_all x1, starting transfers between devices, on_device(): lax.all_to_all(as_sent(shampoo), 'fsdp', split_axis=1, concat_axis=0, til...  10.4 us
    all_to_all x1, starting transfers between devices, on_device(): lax.all_to_all(outgoing, 'fsdp', split_axis=0, concat_axis=1, tiled=True)  10.4 us
  transfers between devices with their start and end apart: 4, of which 4 were waited for; matrix products, arithmetic and copies ran while one was open for 1% of the time, Pallas kernels for 0%

commit v1 on v0

--- a/solution.py
+++ b/solution.py
@@ -83,8 +83,11 @@
     shampoo = batch_product(
         batch_product(inverse_roots[:slot_count], block_float), inverse_roots[slot_count:]
     )
-    returned = lax.all_to_all(
-        as_sent(shampoo), "fsdp", split_axis=1, concat_axis=0, tiled=True
+    returned = jnp.concatenate(
+        lax.all_to_all(
+            jnp.stack(jnp.split(as_sent(shampoo), lax.axis_size("fsdp"), axis=1)), "fsdp", 0, 0
+        ),
+        axis=0,
     ).astype(shampoo.dtype)
     shampoo_rows = jnp.take(returned, block_slot, axis=0)
     shampoo_part = jnp.sum(shampoo_rows * shampoo_rows, axis=(1, 2))

time: 364 us -> 401 us (1.10)
  local copies, waits for them, and re-layouts: 11 us -> 47.2 us
    unnamed x18 -> x81, local copies, waits for them, and re-layouts: 4.93 us -> 42.8 us
where the time goes in v1:
time: 401 us; the launch traced here: 398 us
  waiting for transfers between devices  135 us (34%)
  blocking collectives  126 us (31%)
  local copies, waits for them, and re-layouts  47.2 us (12%)
  matrix products  46.4 us (12%)
  starting transfers between devices  21.5 us (5%)
  between operations  15.4 us (4%)
  other arithmetic  6.66 us (2%)
    psum x1, blocking collectives, on_device(): graft_total, shampoo_total = lax.psum((graft_part, shampoo_part), 'fsdp')  126 us
    psum x1, waiting for transfers between devices, on_device(): lax.psum(grad_blocks[0].astype(jnp.float32).astype(jnp.bfloat16), 'rep')  53.5 us
    unnamed x81, local copies, waits for them, and re-layouts  42.8 us
    dot_general x22, matrix products, batch_product(): jnp.einsum('sij,sjk->sik', left, right, precision=lax.Precision.HIGHEST)  41.6 us
    all_gather x1, waiting for transfers between devices, on_device(): lax.all_gather(batch_root(own_share).astype(jnp.bfloat16), 'rep', axis=0,...  29 us
    all_to_all x1, waiting for transfers between devices, on_device(): lax.all_to_all(outgoing, 'fsdp', split_axis=0, concat_axis=1, tiled=True)  27.6 us
    all_to_all x1, waiting for transfers between devices, on_device(): lax.all_to_all(jnp.stack(jnp.split(as_sent(shampoo), lax.axis_size('fsdp'...  24.6 us
    all_to_all x1, starting transfers between devices, on_device(): lax.all_to_all(jnp.stack(jnp.split(as_sent(shampoo), lax.axis_size('fsdp'...  10.4 us
  transfers between devices with their start and end apart: 4, of which 4 were waited for; matrix products, arithmetic and copies ran while one was open for 1% of the time, Pallas kernels for 0%

profile of v1, /device:TPU:8, one launch (start us, length us, event | category | flops | bytes accessed | tf_op | source)
XLA Modules:
  0.0 397.9 jit_solution(11093587800116326034)
XLA Ops:
  7.2 2.0 copy.45
  9.2 53.5 %all-reduce.4.cloned.1.call-done = (bf16[64,8,512]{2,0,1:T(8,128)(2,1)}, bf16[2,8,8192]{2,1,0:T(8,128)(2,1)}) async-done(((bf16[64,8,512]{2,0,1:T(8,128)(2,1)}, bf16[2,8,8192]{2,1,0:T(8,128)(2,1)}), (bf16[64,8,512]{2,0,1:T(8,128)(2,1)}, bf16[2,8,8192]{2,1,0:T(8,128)(2,1)})) %all-reduce.4.cloned.1.call-update) | async-done | bytes 786448 | tf_op jit(solution)/shard_map/psum | solution.py:41
  65.9 10.4 %all-to-all-start = ((bf16[128,8,512]{2,1,0:T(8,128)(2,1)}), bf16[128,8,512]{2,1,0:T(8,128)(2,1)S(1)}, u32[]{:S(2)}, u32[]{:S(2)}) async-start(bf16[128,8,512]{2,1,0:T(8,128)(2,1)} %copy.24), calls=%async_computation | async-start | bytes 2097152 | tf_op jit(solution)/shard_map/all_to_all | solution.py:67
  77.0 27.6 %all-to-all-done = bf16[128,8,512]{2,1,0:T(8,128)(2,1)S(1)} async-done(((bf16[128,8,512]{2,1,0:T(8,128)(2,1)}), bf16[128,8,512]{2,1,0:T(8,128)(2,1)S(1)}, u32[]{:S(2)}, u32[]{:S(2)}) %all-to-all-start) | async-done | bytes 1048608 | tf_op jit(solution)/shard_map/all_to_all | solution.py:67
  104.5 2.5 convolution_add_fusion
  112.2 1.9 fusion.12
  117.8 2.0 fusion.10
  119.8 1.9 fusion.31
  123.6 2.0 fusion.104
  125.6 1.9 fusion.27
  127.5 1.9 fusion.29
  131.3 1.8 fusion.106
  133.2 1.9 fusion.23
  135.1 1.9 fusion.25
  137.0 2.1 fusion.107
  140.9 1.9 fusion.19
  142.9 1.9 fusion.21
  146.6 1.9 fusion
  148.5 2.6 convolution_convert_fusion.2
  151.2 29.0 %all-gather.3.cloned.1.call-done = bf16[2048,512]{1,0:T(8,128)(2,1)} async-done(((bf16[512,512]{1,0:T(8,128)(2,1)}), bf16[2048,512]{1,0:T(8,128)(2,1)}) %all-gather.3.cloned.1.call-update) | async-done | bytes 2097168 | tf_op jit(solution)/shard_map/all_gather | solution.py:79
  182.6 2.1 convolution_convert_fusion.1
  223.2 10.4 %all-to-all-start.1 = ((bf16[64,2,8,512]{3,2,1,0:T(8,128)(2,1)}), bf16[64,2,8,512]{3,2,1,0:T(8,128)(2,1)S(1)}, u32[]{:S(2)}, u32[]{:S(2)}) async-start(bf16[64,2,8,512]{3,2,1,0:T(8,128)(2,1)} %constant_dynamic-update-slice_fusion), calls=%async_computation.1 | async-start | bytes 2097152 | tf_op jit(solution)/shard_map/all_to_all | solution.py:87
  237.2 24.6 %all-to-all-done.1 = bf16[64,2,8,512]{3,2,1,0:T(8,128)(2,1)S(1)} async-done(((bf16[64,2,8,512]{3,2,1,0:T(8,128)(2,1)}), bf16[64,2,8,512]{3,2,1,0:T(8,128)(2,1)S(1)}, u32[]{:S(2)}, u32[]{:S(2)}) %all-to-all-start.1) | async-done | bytes 1048608 | tf_op jit(solution)/shard_map/all_to_all | solution.py:87
  263.8 126.0 %all-reduce = (f32[64]{0:T(128)S(1)}, f32[64]{0:T(128)S(1)}) all-reduce(f32[64]{0:T(128)S(1)} %multiply_reduce_fusion, f32[64]{0:T(128)S(1)} %get-tuple-element.30), channel_id=1, replica_groups=mesh['rep'=4,'fsdp'=64] {'fsdp'}, use_global_device_ids=true, to_apply=%region_5.6 | all-reduce | flops 128 | bytes 1024 | tf_op jit(solution)/shard_map/psum | solution.py:94
  (108 shorter events, 66.7 us)
Async XLA Ops:
  7.2 55.6 %all-reduce.4.cloned.1.call-start = ((), (), s32[]{:S(2)}) async-start(), calls=%async_computation.3 | async-start | bytes 1572864 | tf_op jit(solution)/shard_map/psum | solution.py:41
  65.9 38.6 %all-to-all-start = ((bf16[128,8,512]{2,1,0:T(8,128)(2,1)}), bf16[128,8,512]{2,1,0:T(8,128)(2,1)S(1)}, u32[]{:S(2)}, u32[]{:S(2)}) async-start(bf16[128,8,512]{2,1,0:T(8,128)(2,1)} %copy.24), calls=%async_computation | async-start | bytes 2097152 | tf_op jit(solution)/shard_map/all_to_all | solution.py:67
  76.4 103.9 %all-gather.3.cloned.1.call-start = ((), (), s32[]{:S(2)}) async-start(), calls=%async_computation.2 | async-start | bytes 2621440 | tf_op jit(solution)/shard_map/all_gather | solution.py:79
  104.5 2.5 copy-start.2
  107.0 3.7 copy-start
  107.8 1.3 copy-start.1
  148.5 2.7 copy-start.7
  184.7 48.9 %copy-start.3 = (bf16[64,8,512]{2,0,1:T(8,128)(2,1)S(1)}, bf16[64,8,512]{2,0,1:T(8,128)(2,1)}, u32[]{:S(2)}) copy-start(bf16[64,8,512]{2,0,1:T(8,128)(2,1)} %get-tuple-element.26) | copy-start | bytes 1572868
  184.7 48.9 %copy-start.4 = (f32[64,8,512]{2,1,0:T(8,128)S(1)}, f32[64,8,512]{2,1,0:T(8,128)}, u32[]{:S(2)}) copy-start(f32[64,8,512]{2,1,0:T(8,128)} %param.8) | copy-start | bytes 3145732
  223.2 38.6 %all-to-all-start.1 = ((bf16[64,2,8,512]{3,2,1,0:T(8,128)(2,1)}), bf16[64,2,8,512]{3,2,1,0:T(8,128)(2,1)S(1)}, u32[]{:S(2)}, u32[]{:S(2)}) async-start(bf16[64,2,8,512]{3,2,1,0:T(8,128)(2,1)} %constant_dynamic-update-slice_fusion), calls=%async_computation.1 | async-start | bytes 2097152 | tf_op jit(solution)/shard_map/all_to_all | solution.py:87
  233.7 2.5 copy-start.5
  233.7 2.5 copy-start.6
Sparse Core Ops, SparseCore 0:
  11.0 51.6 all-reduce.3
  151.3 28.9 all-gather.2
